TPU v7x, 256 devices: a whole 4x4x8 slice. The times are simulated.
256 devices in a mesh: dp: 64 (over z, y, core), tensor: 4 (over x).
Axes of the slice: x: 4, y: 4, z: 8, core: 2. Of those that a mesh axis runs over, the one named last changes fastest.
Arguments:
- gradient: float32 [48, 1024, 1024], P(None, 'dp', 'tensor'), may hold values from -90 to 90
- second_moment: float32 [48, 1024, 1024], P(None, 'dp', 'tensor'), may hold values from 0.1 to 1
- owner_table: int32 [48], replicated, may hold values from 0 to 63, as said below
- slot_table: int32 [48], replicated, may hold values from 0 to 1, as said below
- left_stat: float32 [64, 2, 1024, 1024], P('dp', None, 'tensor'), may hold values from -1 to 4
- right_stat: float32 [64, 2, 1024, 1024], P('dp', None, 'tensor'), may hold values from -1 to 4
- left_root: bfloat16 [64, 2, 1024, 1024], P('dp', None, 'tensor'), may hold values from -1 to 4
- right_root: bfloat16 [64, 2, 1024, 1024], P('dp', None, 'tensor'), may hold values from -1 to 4
Outputs:
- update: bfloat16 [48, 1024, 1024], P(None, 'dp', 'tensor')
- new_second: float32 [48, 1024, 1024], P(None, 'dp', 'tensor')
- left_new: float32 [64, 2, 1024, 1024], P('dp', None, 'tensor')
- right_new: float32 [64, 2, 1024, 1024], P('dp', None, 'tensor')
Inputs may be any that keep to these rules, and one draw needn't show every extreme that they name: The pairs (owner_table[b], slot_table[b]) are distinct; each owner holds at most 2 blocks, and some owner holds exactly 2; owners 0 and 63 each hold at least one block. `slot_table`: paired with owner_table as stated there.
All inputs are finite; a program needn't handle non-finite values.
Results may differ from a plain program's by a relative error of at most 0.0064.
Values may be sent and summed in bfloat16 or wider, within the bound.
A program may use at most 64 MiB of HBM per device.

v0:
```python
import jax
import jax.numpy as jnp
from jax import lax
from jax.sharding import PartitionSpec as P


def per_device(
    gradient, second_moment, owner_table, slot_table, left_stat, right_stat, left_root, right_root
):
    blocks, shard_rows, shard_cols = gradient.shape
    owner_count = lax.axis_size("dp")
    slot_count = left_stat.shape[1]
    stripe = left_stat.shape[2]
    block_order = left_stat.shape[3]
    owner_index = lax.axis_index("dp")
    tensor_index = lax.axis_index("tensor")
    flat_index = owner_table * slot_count + slot_table
    new_second = 0.99 * second_moment + 0.01 * gradient * gradient
    adam = gradient / (jnp.sqrt(new_second) + 1e-08)
    adam_part = jnp.sum(adam * adam, axis=(1, 2))
    grad_low = gradient.astype(jnp.bfloat16)
    gathered = lax.all_gather(grad_low, "tensor", axis=2, tiled=True)
    buffer = (
        jnp.zeros((owner_count * slot_count, shard_rows, block_order), jnp.bfloat16)
        .at[flat_index]
        .set(gathered)
    )
    whole = lax.all_to_all(buffer, "dp", split_axis=0, concat_axis=1, tiled=True)
    row_part = lax.dynamic_slice_in_dim(whole, tensor_index * stripe, stripe, 1)
    col_part = lax.dynamic_slice_in_dim(whole, tensor_index * stripe, stripe, 2)
    left_term = jnp.einsum("sik,sjk->sij", row_part, whole, preferred_element_type=jnp.float32)
    right_term = jnp.einsum("ski,skj->sij", col_part, whole, preferred_element_type=jnp.float32)
    left_new = 0.5 * left_stat + 0.5 / block_order * left_term[None]
    right_new = 0.5 * right_stat + 0.5 / block_order * right_term[None]
    mixed = jnp.einsum(
        "sik,skj->sij", left_root[0], whole, preferred_element_type=jnp.float32
    ).astype(jnp.bfloat16)
    product = jnp.einsum(
        "sik,skj->sij",
        mixed,
        lax.all_gather(right_root[0], "tensor", axis=1, tiled=True),
        preferred_element_type=jnp.float32,
    )
    precond = product.astype(jnp.bfloat16)
    precond_wide = precond.astype(jnp.float32)
    root_slot = jnp.sum(precond_wide * precond_wide, axis=(1, 2))
    returned = lax.all_to_all(
        lax.all_to_all(precond, "tensor", split_axis=2, concat_axis=1, tiled=True),
        "dp",
        split_axis=1,
        concat_axis=0,
        tiled=True,
    )
    returned_blocks = returned[flat_index]
    slot_match = slot_table[:, None] == jnp.arange(slot_count, dtype=jnp.int32)[None, :]
    looked_up = jnp.sum(jnp.where(slot_match, root_slot[None, :], 0.0), axis=1)
    root_part = jnp.where(owner_table == owner_index, looked_up, 0.0)
    adam_total, root_total = lax.psum((adam_part, root_part), ("dp", "tensor"))
    graft_scale = jnp.sqrt(adam_total / (root_total + 1e-06))
    update = (graft_scale[:, None, None] * returned_blocks.astype(jnp.float32)).astype(jnp.bfloat16)
    return (update, new_second, left_new, right_new)


def solution(mesh):
    placed = (
        P(None, "dp", "tensor"),
        P(None, "dp", "tensor"),
        P(),
        P(),
        P("dp", None, "tensor", None),
        P("dp", None, "tensor", None),
        P("dp", None, "tensor", None),
        P("dp", None, "tensor", None),
    )
    return jax.shard_map(
        per_device,
        mesh=mesh,
        in_specs=placed,
        out_specs=(
            P(None, "dp", "tensor"),
            P(None, "dp", "tensor"),
            P("dp", None, "tensor", None),
            P("dp", None, "tensor", None),
        ),
        check_vma=False,
    )
```

profile of v0, /device:TPU:1, one launch (start us, length us, event | category | flops | bytes accessed | tf_op | source)
XLA Modules:
  0.0 296.8 jit_solution(7836436570167904347)
XLA Ops:
  7.2 0.0 copy-start
  7.2 0.0 copy-start.4
  7.2 0.0 copy-start.5
  7.2 0.0 all-gather.4.cloned.1.call-start
  7.2 3.2 %multiply_reduce_fusion.1 = (f32[48]{0:T(128)S(1)}, f32[48,16,256]{2,1,0:T(8,128)}, bf16[48,16,256]{2,1,0:T(8,128)(2,1)}) fusion(f32[48,16,256]{2,1,0:T(8,128)} %param.8, f32[48,16,256]{2,1,0:T(8,128)} %param.9), kind=kLoop, calls=%fused_computation.15 | loop fusion | flops 1769424 | bytes 2752704 | tf_op jit(solution)/shard_map/reduce_sum | solution.py:20
  10.4 0.0 all-gather.4.cloned.1.call-update
  10.5 0.0 copy-done.4
  10.5 0.0 copy-done.5
  10.5 34.7 %all-gather.4.cloned.1.call-done = bf16[48,16,1024]{2,1,0:T(8,128)(2,1)} async-done(((bf16[48,16,256]{2,1,0:T(8,128)(2,1)}), bf16[48,16,1024]{2,1,0:T(8,128)(2,1)}) %all-gather.4.cloned.1.call-update) | async-done | bytes 1572880 | tf_op jit(solution)/shard_map/all_gather | solution.py:22
  45.2 0.0 copy-start.3
  45.2 2.5 broadcast_in_dim.29
  47.7 0.0 copy-done.3
  47.7 6.6 %scatter_fusion = bf16[128,16,1024]{2,1,0:T(8,128)(2,1)} fusion(bf16[128,16,1024]{2,1,0:T(8,128)(2,1)} %broadcast_in_dim.29, s32[48]{0:T(128)S(1)} %compare_select_fusion, bf16[48,16,1024]{2,1,0:T(8,128)(2,1)S(1)} %copy-done.3), kind=kCustom, calls=%fused_computation.1 | custom fusion | bytes 4718784 | tf_op jit(solution)/shard_map/scatter | solution.py:26
  54.3 12.2 %all-to-all-start = ((bf16[128,16,1024]{2,1,0:T(8,128)(2,1)}), bf16[128,16,1024]{2,1,0:T(8,128)(2,1)}, u32[]{:S(2)}, u32[]{:S(2)}) async-start(bf16[128,16,1024]{2,1,0:T(8,128)(2,1)} %scatter_fusion), calls=%async_computation | async-start | bytes 8388608 | tf_op jit(solution)/shard_map/all_to_all | solution.py:28
  66.5 0.0 all-gather.6.cloned.1.call-start
  66.6 0.7 all-gather.6.cloned.1.call-update
  67.3 94.0 %all-to-all-done = bf16[128,16,1024]{2,1,0:T(8,128)(2,1)} async-done(((bf16[128,16,1024]{2,1,0:T(8,128)(2,1)}), bf16[128,16,1024]{2,1,0:T(8,128)(2,1)}, u32[]{:S(2)}, u32[]{:S(2)}) %all-to-all-start) | async-done | bytes 4194336 | tf_op jit(solution)/shard_map/all_to_all | solution.py:28
  161.2 5.0 %copy.34 = bf16[2,64,16,1024]{3,2,1,0:T(8,128)(2,1)} copy(bf16[2,64,16,1024]{3,2,0,1:T(8,128)(2,1)} %bitcast.1) | data formatting | bytes 8388608 | tf_op jit(solution)/shard_map/all_to_all | solution.py:28
  166.2 0.0 all-gather.6.cloned.1.call-done
  166.2 0.0 copy-done
  166.2 6.1 %multiply_reduce_fusion = (f32[2]{0:T(128)S(1)}, bf16[2,256,1024]{2,1,0:T(8,128)(2,1)S(1)}) fusion(bf16[1,2,1024,1024]{3,2,1,0:T(8,128)(2,1)} %all-gather.6.cloned.1.call-done, bf16[2,1024,1024]{2,1,0:T(8,128)(2,1)} %bitcast.33, bf16[1,2,256,1024]{3,2,1,0:T(8,128)(2,1)S(1)} %copy-done), kind=kOutput, calls=%fused_computation.6 | convolution fusion | flops 2150105088 | bytes 10485768 | tf_op jit(solution)/shard_map/sik,skj->sij/dot_general | solution.py:38
  172.4 0.9 copy.37
  173.3 16.3 %all_to_all.54 = bf16[2,256,1024]{1,0,2:T(2,128)(2,1)S(1)} all-to-all(bf16[2,256,1024]{1,0,2:T(2,128)(2,1)S(1)} %copy.37), channel_id=1, replica_groups=mesh['dp'=64,'tensor'=4] {'tensor'}, dimensions={2} | all-to-all | bytes 2097152 | tf_op jit(solution)/shard_map/all_to_all | solution.py:48
  189.6 0.1 copy.38
  189.8 0.5 copy.39
  190.3 2.1 copy.40
  192.3 9.4 %all-to-all-start.2 = ((bf16[2,1024,256]{2,0,1:T(2,128)(2,1)}), bf16[2,1024,256]{2,0,1:T(2,128)(2,1)S(1)}, u32[]{:S(2)}, u32[]{:S(2)}) async-start(bf16[2,1024,256]{2,0,1:T(2,128)(2,1)} %copy.40), calls=%async_computation.2 | async-start | bytes 2097152 | tf_op jit(solution)/shard_map/all_to_all | solution.py:47
  201.8 0.1 fusion.11
  201.9 77.7 %all-reduce = (f32[48]{0:T(128)S(1)}, f32[48]{0:T(128)S(1)}) all-reduce(f32[48]{0:T(128)S(1)} %get-tuple-element.6, f32[48]{0:T(128)S(1)} %compare_select_fusion.2), channel_id=1, replica_groups=mesh['dp'=64,'tensor'=4] {'dp','tensor'}, use_global_device_ids=true, to_apply=%region_1.0 | all-reduce | flops 96 | bytes 768 | tf_op jit(solution)/shard_map/psum | solution.py:58
  279.6 0.0 copy-start.1
  279.6 0.0 copy-start.2
  279.6 6.0 %bitcast_add_fusion = f32[1,2,256,1024]{3,2,1,0:T(8,128)} fusion(f32[1,2,256,1024]{3,2,1,0:T(8,128)} %param.13, bf16[2,1024,1024]{2,1,0:T(8,128)(2,1)} %bitcast.34, s32[]{:T(128)S(6)} %select_n.19), kind=kOutput, calls=%fused_computation.4 | convolution fusion | flops 1075314688 | bytes 9437188 | tf_op jit(solution)/shard_map/ski,skj->sij/dot_general | solution.py:32
  285.6 0.0 copy-done.1
  285.6 0.0 copy-done.2
  285.6 2.7 bitcast_add_fusion.1
  288.3 0.0 all-to-all-done.2
  288.3 0.1 copy.41
  288.4 0.1 copy.42
  288.5 0.6 gather_fusion
  289.1 0.9 multiply_convert_fusion
  (4 shorter events, 0.0 us)
Async XLA Ops:
  7.2 159.1 %copy-start = (bf16[1,2,256,1024]{3,2,1,0:T(8,128)(2,1)S(1)}, bf16[1,2,256,1024]{3,2,1,0:T(8,128)(2,1)}, u32[]{:S(2)}) copy-start(bf16[1,2,256,1024]{3,2,1,0:T(8,128)(2,1)} %param.14) | copy-start | bytes 3145732
  7.2 3.3 %copy-start.4 = (s32[48]{0:T(128)S(1)}, s32[48]{0:T(128)}, u32[]{:S(2)}) copy-start(s32[48]{0:T(128)} %param.10) | copy-start | bytes 580
  7.2 3.3 %copy-start.5 = (s32[48]{0:T(128)S(1)}, s32[48]{0:T(128)}, u32[]{:S(2)}) copy-start(s32[48]{0:T(128)} %param.11) | copy-start | bytes 580
  7.2 38.0 %all-gather.4.cloned.1.call-start = ((), (), s32[]{:S(2)}) async-start(), calls=%async_computation.3 | async-start | bytes 1966080 | tf_op jit(solution)/shard_map/all_gather | solution.py:22
  45.2 2.5 copy-start.3
  54.3 107.0 %all-to-all-start = ((bf16[128,16,1024]{2,1,0:T(8,128)(2,1)}), bf16[128,16,1024]{2,1,0:T(8,128)(2,1)}, u32[]{:S(2)}, u32[]{:S(2)}) async-start(bf16[128,16,1024]{2,1,0:T(8,128)(2,1)} %scatter_fusion), calls=%async_computation | async-start | bytes 8388608 | tf_op jit(solution)/shard_map/all_to_all | solution.py:28
  66.5 99.7 %all-gather.6.cloned.1.call-start = ((), (), s32[]{:S(2)}) async-start(), calls=%async_computation.4 | async-start | bytes 5242880 | tf_op jit(solution)/shard_map/all_gather | solution.py:41
  192.3 95.9 %all-to-all-start.2 = ((bf16[2,1024,256]{2,0,1:T(2,128)(2,1)}), bf16[2,1024,256]{2,0,1:T(2,128)(2,1)S(1)}, u32[]{:S(2)}, u32[]{:S(2)}) async-start(bf16[2,1024,256]{2,0,1:T(2,128)(2,1)} %copy.40), calls=%async_computation.2 | async-start | bytes 2097152 | tf_op jit(solution)/shard_map/all_to_all | solution.py:47
  279.6 6.0 %copy-start.1 = (bf16[2,64,16,1024]{3,2,1,0:T(8,128)(2,1)S(1)}, bf16[2,64,16,1024]{3,2,1,0:T(8,128)(2,1)}, u32[]{:S(2)}) copy-start(bf16[2,64,16,1024]{3,2,1,0:T(8,128)(2,1)} %copy.34) | copy-start | bytes 12582916
  279.6 6.0 %copy-start.2 = (f32[1,2,256,1024]{3,2,1,0:T(8,128)S(1)}, f32[1,2,256,1024]{3,2,1,0:T(8,128)}, u32[]{:S(2)}) copy-start(f32[1,2,256,1024]{3,2,1,0:T(8,128)} %param.12) | copy-start | bytes 6291460
Sparse Core Ops, SparseCore 0:
  10.6 34.5 all-gather.3
  69.2 51.1 all-gather.5
where the time goes:
time: 297 us
  waiting for transfers between devices  129 us (43%)
  blocking collectives  94 us (32%)
  starting transfers between devices  21.7 us (7%)
  local copies, waits for them, and re-layouts  18.6 us (6%)
  matrix products  14.8 us (5%)
  between operations  14.2 us (5%)
  other arithmetic  4.19 us (1%)
    all_to_all x1, waiting for transfers between devices, per_device(): lax.all_to_all(buffer, 'dp', split_axis=0, concat_axis=1, tiled=True)  94 us
    psum x1, blocking collectives, per_device(): adam_total, root_total = lax.psum((adam_part, root_part), ('dp', 'tensor'))  77.7 us
    all_gather x1, waiting for transfers between devices, per_device(): gathered = lax.all_gather(grad_low, 'tensor', axis=2, tiled=True)  34.7 us
    all_to_all x1, blocking collectives, per_device(): lax.all_to_all(precond, 'tensor', split_axis=2, concat_axis=1, tiled=True)  16.3 us
    all_to_all x1, starting transfers between devices, per_device(): lax.all_to_all(buffer, 'dp', split_axis=0, concat_axis=1, tiled=True)  12.2 us
    all_to_all x1, starting transfers between devices, per_device(): lax.all_to_all(lax.all_to_all(precond, 'tensor', split_axis=2, concat_axi...  9.43 us
    scatter x1, local copies, waits for them, and re-layouts, per_device(): buffer = jnp.zeros((owner_count * slot_count, shard_rows, block_order), j...  6.59 us
    dot_general x1, matrix products, per_device(): jnp.einsum('sik,skj->sij', mixed, lax.all_gather(right_root[0], 'tensor',...  6.14 us
  transfers between devices with their start and end apart: 4, of which 2 were waited for; matrix products, arithmetic and copies ran while one was open for 5% of the time, Pallas kernels for 0%

commit v1 on v0

--- a/solution.py
+++ b/solution.py
@@ -55,7 +55,7 @@
     slot_match = slot_table[:, None] == jnp.arange(slot_count, dtype=jnp.int32)[None, :]
     looked_up = jnp.sum(jnp.where(slot_match, root_slot[None, :], 0.0), axis=1)
     root_part = jnp.where(owner_table == owner_index, looked_up, 0.0)
-    adam_total, root_total = lax.psum((adam_part, root_part), ("dp", "tensor"))
+    adam_total, root_total = lax.psum(lax.psum((adam_part, root_part), "dp"), "tensor")
     graft_scale = jnp.sqrt(adam_total / (root_total + 1e-06))
     update = (graft_scale[:, None, None] * returned_blocks.astype(jnp.float32)).astype(jnp.bfloat16)
     return (update, new_second, left_new, right_new)

time: 297 us -> 371 us (1.25)
  blocking collectives: 94 us -> 164 us
    psum x1 -> x2, blocking collectives: 77.7 us -> 148 us  [the longest x1 141 us: per_device(): lax.psum((adam_part, root_part), 'dp')]
  transfers between devices with their start and end apart: 4 -> 4, of which waited for: 2 -> 2; matrix products, arithmetic and copies ran while one was open for 5% -> 4% of each run, Pallas kernels for 0% -> 0%
where the time goes in v1:
time: 371 us; the launch traced here: 367 us
  blocking collectives  164 us (44%)
  waiting for transfers between devices  129 us (35%)
  starting transfers between devices  21.8 us (6%)
  local copies, waits for them, and re-layouts  18.6 us (5%)
  matrix products  14.8 us (4%)
  between operations  14.2 us (4%)
  other arithmetic  4.19 us (1%)
    psum x1, blocking collectives, per_device(): lax.psum((adam_part, root_part), 'dp')  141 us
    all_to_all x1, waiting for transfers between devices, per_device(): lax.all_to_all(buffer, 'dp', split_axis=0, concat_axis=1, tiled=True)  94 us
    all_gather x1, waiting for transfers between devices, per_device(): gathered = lax.all_gather(grad_low, 'tensor', axis=2, tiled=True)  34.7 us
    all_to_all x1, blocking collectives, per_device(): lax.all_to_all(precond, 'tensor', split_axis=2, concat_axis=1, tiled=True)  16.3 us
    all_to_all x1, starting transfers between devices, per_device(): lax.all_to_all(buffer, 'dp', split_axis=0, concat_axis=1, tiled=True)  12.2 us
    all_to_all x1, starting transfers between devices, per_device(): lax.all_to_all(lax.all_to_all(precond, 'tensor', split_axis=2, concat_axi...  9.43 us
  transfers between devices with their start and end apart: 4, of which 2 were waited for; matrix products, arithmetic and copies ran while one was open for 4% of the time, Pallas kernels for 0%

profile of v1, /device:TPU:1, one launch (start us, length us, event | category | flops | bytes accessed | tf_op | source)
XLA Modules:
  0.0 367.4 jit_solution(11203289321604169583)
XLA Ops:
  7.2 0.0 copy-start
  7.2 0.0 copy-start.4
  7.2 0.0 copy-start.5
  7.2 0.0 all-gather.4.cloned.1.call-start
  7.2 3.2 multiply_reduce_fusion.1
  10.4 0.0 all-gather.4.cloned.1.call-update
  10.5 0.0 copy-done.4
  10.5 0.0 copy-done.5
  10.5 34.7 %all-gather.4.cloned.1.call-done = bf16[48,16,1024]{2,1,0:T(8,128)(2,1)} async-done(((bf16[48,16,256]{2,1,0:T(8,128)(2,1)}), bf16[48,16,1024]{2,1,0:T(8,128)(2,1)}) %all-gather.4.cloned.1.call-update) | async-done | bytes 1572880 | tf_op jit(solution)/shard_map/all_gather | solution.py:22
  45.2 0.0 copy-start.3
  45.2 2.5 broadcast_in_dim.29
  47.7 0.0 copy-done.3
  47.7 6.6 %scatter_fusion = bf16[128,16,1024]{2,1,0:T(8,128)(2,1)} fusion(bf16[128,16,1024]{2,1,0:T(8,128)(2,1)} %broadcast_in_dim.29, s32[48]{0:T(128)S(1)} %compare_select_fusion, bf16[48,16,1024]{2,1,0:T(8,128)(2,1)S(1)} %copy-done.3), kind=kCustom, calls=%fused_computation.1 | custom fusion | bytes 4718784 | tf_op jit(solution)/shard_map/scatter | solution.py:26
  54.3 12.2 %all-to-all-start = ((bf16[128,16,1024]{2,1,0:T(8,128)(2,1)}), bf16[128,16,1024]{2,1,0:T(8,128)(2,1)}, u32[]{:S(2)}, u32[]{:S(2)}) async-start(bf16[128,16,1024]{2,1,0:T(8,128)(2,1)} %scatter_fusion), calls=%async_computation | async-start | bytes 8388608 | tf_op jit(solution)/shard_map/all_to_all | solution.py:28
  66.6 0.0 all-gather.6.cloned.1.call-start
  66.6 0.7 all-gather.6.cloned.1.call-update
  67.3 94.0 %all-to-all-done = bf16[128,16,1024]{2,1,0:T(8,128)(2,1)} async-done(((bf16[128,16,1024]{2,1,0:T(8,128)(2,1)}), bf16[128,16,1024]{2,1,0:T(8,128)(2,1)}, u32[]{:S(2)}, u32[]{:S(2)}) %all-to-all-start) | async-done | bytes 4194336 | tf_op jit(solution)/shard_map/all_to_all | solution.py:28
  161.3 5.0 %copy.34 = bf16[2,64,16,1024]{3,2,1,0:T(8,128)(2,1)} copy(bf16[2,64,16,1024]{3,2,0,1:T(8,128)(2,1)} %bitcast.1) | data formatting | bytes 8388608 | tf_op jit(solution)/shard_map/all_to_all | solution.py:28
  166.2 0.0 all-gather.6.cloned.1.call-done
  166.2 0.0 copy-done
  166.2 6.1 %multiply_reduce_fusion = (f32[2]{0:T(128)S(1)}, bf16[2,256,1024]{2,1,0:T(8,128)(2,1)S(1)}) fusion(bf16[1,2,1024,1024]{3,2,1,0:T(8,128)(2,1)} %all-gather.6.cloned.1.call-done, bf16[2,1024,1024]{2,1,0:T(8,128)(2,1)} %bitcast.33, bf16[1,2,256,1024]{3,2,1,0:T(8,128)(2,1)S(1)} %copy-done), kind=kOutput, calls=%fused_computation.6 | convolution fusion | flops 2150105088 | bytes 10485768 | tf_op jit(solution)/shard_map/sik,skj->sij/dot_general | solution.py:38
  172.4 0.9 copy.37
  173.3 16.3 %all_to_all.54 = bf16[2,256,1024]{1,0,2:T(2,128)(2,1)S(1)} all-to-all(bf16[2,256,1024]{1,0,2:T(2,128)(2,1)S(1)} %copy.37), channel_id=1, replica_groups=mesh['dp'=64,'tensor'=4] {'tensor'}, dimensions={2} | all-to-all | bytes 2097152 | tf_op jit(solution)/shard_map/all_to_all | solution.py:48
  189.6 0.1 copy.38
  189.8 0.5 copy.39
  190.3 2.0 copy.40
  192.4 9.4 %all-to-all-start.2 = ((bf16[2,1024,256]{2,0,1:T(2,128)(2,1)}), bf16[2,1024,256]{2,0,1:T(2,128)(2,1)S(1)}, u32[]{:S(2)}, u32[]{:S(2)}) async-start(bf16[2,1024,256]{2,0,1:T(2,128)(2,1)} %copy.40), calls=%async_computation.2 | async-start | bytes 2097152 | tf_op jit(solution)/shard_map/all_to_all | solution.py:47
  201.8 0.1 fusion.11
  201.9 141.3 %all-reduce = (f32[48]{0:T(128)S(1)}, f32[48]{0:T(128)S(1)}) all-reduce(f32[48]{0:T(128)S(1)} %get-tuple-element.8, f32[48]{0:T(128)S(1)} %compare_select_fusion.2), channel_id=1, replica_groups=mesh['dp'=64,'tensor'=4] {'dp'}, use_global_device_ids=true, to_apply=%region_1.0 | all-reduce | flops 96 | bytes 768 | tf_op jit(solution)/shard_map/psum | solution.py:58
  343.2 6.9 %all-reduce.1 = (f32[48]{0:T(128)S(1)}, f32[48]{0:T(128)S(1)}) all-reduce(f32[48]{0:T(128)S(1)} %get-tuple-element.4, f32[48]{0:T(128)S(1)} %get-tuple-element.5), channel_id=1, replica_groups=mesh['dp'=64,'tensor'=4] {'tensor'}, use_global_device_ids=true, to_apply=%region_2.0 | all-reduce | flops 96 | bytes 768 | tf_op jit(solution)/shard_map/psum | solution.py:58
  350.1 0.0 copy-start.1
  350.1 0.0 copy-start.2
  350.1 6.0 %bitcast_add_fusion = f32[1,2,256,1024]{3,2,1,0:T(8,128)} fusion(f32[1,2,256,1024]{3,2,1,0:T(8,128)} %param.13, bf16[2,1024,1024]{2,1,0:T(8,128)(2,1)} %bitcast.34, s32[]{:T(128)S(6)} %select_n.19), kind=kOutput, calls=%fused_computation.4 | convolution fusion | flops 1075314688 | bytes 9437188 | tf_op jit(solution)/shard_map/ski,skj->sij/dot_general | solution.py:32
  356.1 0.0 copy-done.1
  356.1 0.0 copy-done.2
  356.1 2.7 bitcast_add_fusion.1
  358.8 0.0 all-to-all-done.2
  358.8 0.1 copy.41
  359.0 0.1 copy.42
  359.1 0.6 gather_fusion
  359.7 0.9 multiply_convert_fusion
  (4 shorter events, 0.0 us)
Async XLA Ops:
  7.2 159.1 %copy-start = (bf16[1,2,256,1024]{3,2,1,0:T(8,128)(2,1)S(1)}, bf16[1,2,256,1024]{3,2,1,0:T(8,128)(2,1)}, u32[]{:S(2)}) copy-start(bf16[1,2,256,1024]{3,2,1,0:T(8,128)(2,1)} %param.14) | copy-start | bytes 3145732
  7.2 3.3 copy-start.4
  7.2 3.3 copy-start.5
  7.2 38.0 %all-gather.4.cloned.1.call-start = ((), (), s32[]{:S(2)}) async-start(), calls=%async_computation.3 | async-start | bytes 1966080 | tf_op jit(solution)/shard_map/all_gather | solution.py:22
  45.2 2.5 copy-start.3
  54.3 107.0 %all-to-all-start = ((bf16[128,16,1024]{2,1,0:T(8,128)(2,1)}), bf16[128,16,1024]{2,1,0:T(8,128)(2,1)}, u32[]{:S(2)}, u32[]{:S(2)}) async-start(bf16[128,16,1024]{2,1,0:T(8,128)(2,1)} %scatter_fusion), calls=%async_computation | async-start | bytes 8388608 | tf_op jit(solution)/shard_map/all_to_all | solution.py:28
  66.6 99.7 %all-gather.6.cloned.1.call-start = ((), (), s32[]{:S(2)}) async-start(), calls=%async_computation.4 | async-start | bytes 5242880 | tf_op jit(solution)/shard_map/all_gather | solution.py:41
  192.4 166.4 %all-to-all-start.2 = ((bf16[2,1024,256]{2,0,1:T(2,128)(2,1)}), bf16[2,1024,256]{2,0,1:T(2,128)(2,1)S(1)}, u32[]{:S(2)}, u32[]{:S(2)}) async-start(bf16[2,1024,256]{2,0,1:T(2,128)(2,1)} %copy.40), calls=%async_computation.2 | async-start | bytes 2097152 | tf_op jit(solution)/shard_map/all_to_all | solution.py:47
  350.1 6.0 %copy-start.1 = (bf16[2,64,16,1024]{3,2,1,0:T(8,128)(2,1)S(1)}, bf16[2,64,16,1024]{3,2,1,0:T(8,128)(2,1)}, u32[]{:S(2)}) copy-start(bf16[2,64,16,1024]{3,2,1,0:T(8,128)(2,1)} %copy.34) | copy-start | bytes 12582916
  350.1 6.0 %copy-start.2 = (f32[1,2,256,1024]{3,2,1,0:T(8,128)S(1)}, f32[1,2,256,1024]{3,2,1,0:T(8,128)}, u32[]{:S(2)}) copy-start(f32[1,2,256,1024]{3,2,1,0:T(8,128)} %param.12) | copy-start | bytes 6291460
Sparse Core Ops, SparseCore 0:
  10.6 34.5 all-gather.3
  69.2 51.1 all-gather.5
